TPU v7x, 1024 devices: a whole 4x4x32 slice. The times are simulated.
1024 devices in a mesh: row: 32 (over z), col: 32 (over y, x, core).
Axes of the slice: x: 4, y: 4, z: 32, core: 2. Of those that a mesh axis runs over, the one named last changes fastest.
Arguments:
- amplitudes: bfloat16 [32, 256, 64, 2048], P(None, 'col', 'row'), may hold values from -6 to 6
- integrals: bfloat16 [8, 64, 32, 64], P(None, None, 'col'), may hold values from -0.125 to 0.125
- others: bfloat16 [8, 256, 64, 2048], P(None, 'col', 'row'), may hold values from -6 to 6
- occupied_left: float32 [8], replicated, may hold values from -1.5 to -0.3
- occupied_right: float32 [256], P('col'), may hold values from -1.5 to -0.3
- virtual_left: float32 [64], P('row'), may hold values from 0.2 to 3
- virtual_right: float32 [2048], replicated, may hold values from 0.2 to 3
- tile_mask: int32 [4, 32], replicated, may hold values 0 or 1
Outputs:
- update: bfloat16 [8, 256, 64, 2048], P(None, 'col', 'row')
All inputs are finite; a program needn't handle non-finite values.
Results may differ from a plain program's by a relative error of at most 0.0039.
Values may be sent and summed in bfloat16 or wider, within the bound.
No kernel may reach another device: no remote copies, remote signals or barrier semaphores. Data moves between devices by JAX's collectives and lax.ppermute only.
A program may use at most 64 MiB of HBM per device.

v0:
```python
import jax
import jax.numpy as jnp
from jax import lax
from jax.sharding import PartitionSpec as P

TILE = 64


def contract(panel, amp_rows):
    return jnp.einsum("iakc,kjcb->ijab", panel, amp_rows, preferred_element_type=jnp.float32)


def shards(
    amplitudes,
    integrals,
    others,
    occupied_left,
    occupied_right,
    virtual_left,
    virtual_right,
    tile_mask,
):
    regrouped = lax.all_to_all(amplitudes, "row", split_axis=3, concat_axis=2, tiled=True)
    panels_all = lax.all_gather(integrals, "col", axis=2, tiled=True)
    cycle_term = contract(panels_all, regrouped)
    cycle_half = cycle_term.astype(jnp.bfloat16)
    returned = lax.all_to_all(cycle_half, "row", split_axis=2, concat_axis=3, tiled=True)
    tile_count = tile_mask.shape[0]
    first_pair = lax.axis_index("col") * returned.shape[1]
    pair_ids = first_pair + jnp.arange(returned.shape[1], dtype=jnp.int32)
    select = (pair_ids[:, None] // TILE == jnp.arange(tile_count, dtype=jnp.int32)[None, :]).astype(
        jnp.float32
    )
    mask_rows = jnp.dot(select, tile_mask.astype(jnp.float32))
    keep = jnp.repeat(mask_rows, TILE, axis=1)
    denominator = (
        occupied_left[:, None, None, None]
        + occupied_right[None, :, None, None]
        - virtual_left[None, None, :, None]
        - virtual_right[None, None, None, :]
    )
    result = (
        keep[None, :, None, :]
        * (others.astype(jnp.float32) + returned.astype(jnp.float32))
        / denominator
    )
    return result.astype(jnp.bfloat16)


def solution(mesh):
    in_specs = (
        P(None, "col", "row", None),
        P(None, None, "col", None),
        P(None, "col", "row", None),
        P(),
        P("col"),
        P("row"),
        P(),
        P(),
    )
    out_specs = P(None, "col", "row", None)
    return jax.shard_map(shards, mesh=mesh, in_specs=in_specs, out_specs=out_specs, check_vma=False)
```

profile of v0, /device:TPU:1, one launch (start us, length us, event | category | flops | bytes accessed | tf_op | source)
XLA Modules:
  0.0 372.4 jit_solution(7124757294506612385)
XLA Ops:
  6.5 14.1 %copy.30 = bf16[32,8,2,2048]{0,1,2,3:T(8,128)(2,1)} copy(bf16[32,8,2,2048]{3,2,1,0:T(2,128)(2,1)} %param.8) | data formatting | bytes 4194304 | tf_op args[0]
  20.6 13.3 %reshape.87 = bf16[32,2,16384]{2,1,0:T(2,128)(2,1)} reshape(bf16[2048,2,8,32]{3,2,1,0:T(8,128)(2,1)} %bitcast.34) | data formatting | bytes 4194304
  34.0 29.3 %all-to-all-start = ((bf16[32,2,16384]{2,1,0:T(2,128)(2,1)}), bf16[32,2,16384]{2,1,0:T(2,128)(2,1)S(1)}, u32[]{:S(2)}, u32[]{:S(2)}) async-start(bf16[32,2,16384]{2,1,0:T(2,128)(2,1)} %reshape.87), calls=%async_computation | async-start | bytes 4194304 | tf_op jit(solution)/shard_map/all_to_all | solution.py:23
  63.3 0.0 all-gather.2.cloned.1.call-start
  63.3 0.7 all-gather.2.cloned.1.call-update
  64.0 191.5 %all-to-all-done = bf16[32,2,16384]{2,1,0:T(2,128)(2,1)S(1)} async-done(((bf16[32,2,16384]{2,1,0:T(2,128)(2,1)}), bf16[32,2,16384]{2,1,0:T(2,128)(2,1)S(1)}, u32[]{:S(2)}, u32[]{:S(2)}) %all-to-all-start) | async-done | bytes 2097184 | tf_op jit(solution)/shard_map/all_to_all | solution.py:23
  255.5 6.5 %reshape.88 = bf16[2048,2,8,32]{3,2,1,0:T(8,128)(2,1)} reshape(bf16[32,2,16384]{2,1,0:T(2,128)(2,1)S(1)} %all-to-all-done) | data formatting | bytes 4194304
  262.0 12.8 %copy.32 = bf16[32,8,32,2,64]{4,1,3,2,0:T(8,128)(2,1)} copy(bf16[32,8,32,2,64]{0,1,3,4,2:T(8,128)(2,1)} %bitcast.33) | data formatting | bytes 4194304 | tf_op jit(solution)/shard_map/all_to_all | solution.py:23
  274.9 0.0 all-gather.2.cloned.1.call-done
  274.9 7.6 %fusion.7 = bf16[8,8,64,64]{2,3,0,1:T(8,128)(2,1)S(1)} fusion(bf16[8,64,32,64]{3,1,2,0:T(8,128)(2,1)} %all-gather.2.cloned.1.call-done, bf16[32,8,64,64,1]{3,1,2,0,4:T(8,128)(2,1)} %bitcast.35), kind=kOutput, calls=%fused_computation.5 | convolution fusion | flops 1074003968 | bytes 4718592 | tf_op jit(solution)/shard_map/iakc,kjcb->ijab/dot_general | solution.py:10
  282.5 0.0 copy-start.4
  282.5 0.0 copy-start.1
  282.5 0.0 copy-start.2
  282.5 0.0 copy-start.3
  282.5 1.6 copy.34
  284.2 1.5 reshape.89
  285.7 10.4 %all-to-all-start.1 = ((bf16[32,2,4096]{2,1,0:T(2,128)(2,1)}), bf16[32,2,4096]{2,1,0:T(2,128)(2,1)S(1)}, u32[]{:S(2)}, u32[]{:S(2)}) async-start(bf16[32,2,4096]{2,1,0:T(2,128)(2,1)} %reshape.89), calls=%async_computation.1 | async-start | bytes 1048576 | tf_op jit(solution)/shard_map/all_to_all | solution.py:27
  296.2 0.0 copy-done.4
  296.2 0.2 fusion.12
  296.4 0.1 broadcast_in_dim.2
  296.5 0.1 mul.14
  296.6 0.0 copy-done.1
  296.6 0.0 copy-done.2
  296.6 0.1 broadcast_add_fusion
  296.6 0.0 copy-done.3
  296.6 0.1 broadcast_subtract_fusion
  296.7 63.8 %all-to-all-done.1 = bf16[32,2,4096]{2,1,0:T(2,128)(2,1)S(1)} async-done(((bf16[32,2,4096]{2,1,0:T(2,128)(2,1)}), bf16[32,2,4096]{2,1,0:T(2,128)(2,1)S(1)}, u32[]{:S(2)}, u32[]{:S(2)}) %all-to-all-start.1) | async-done | bytes 524320 | tf_op jit(solution)/shard_map/all_to_all | solution.py:27
  360.5 0.7 reshape.90
  361.1 0.1 copy.35
  361.3 0.2 convert_bitcast_fusion
  361.5 0.0 copy-start
  361.5 0.6 copy.36
  362.1 0.7 reshape.82
  362.8 0.0 copy-done
  362.8 1.4 divide_convert_fusion
  364.2 1.3 copy.37
  (1 shorter events, 0.0 us)
Async XLA Ops:
  34.0 221.6 %all-to-all-start = ((bf16[32,2,16384]{2,1,0:T(2,128)(2,1)}), bf16[32,2,16384]{2,1,0:T(2,128)(2,1)S(1)}, u32[]{:S(2)}, u32[]{:S(2)}) async-start(bf16[32,2,16384]{2,1,0:T(2,128)(2,1)} %reshape.87), calls=%async_computation | async-start | bytes 4194304 | tf_op jit(solution)/shard_map/all_to_all | solution.py:23
  63.3 211.6 %all-gather.2.cloned.1.call-start = ((), (), s32[]{:S(2)}) async-start(), calls=%async_computation.2 | async-start | bytes 4325376 | tf_op jit(solution)/shard_map/all_gather | solution.py:24
  282.5 13.7 %copy-start.4 = (s32[4,32]{1,0:T(4,128)S(1)}, s32[4,32]{1,0:T(4,128)}, u32[]{:S(2)}) copy-start(s32[4,32]{1,0:T(4,128)} %param.15) | copy-start | bytes 1540
  282.5 14.1 %copy-start.1 = (f32[8]{0:T(128)S(1)}, f32[8]{0:T(128)}, u32[]{:S(2)}) copy-start(f32[8]{0:T(128)} %param.12) | copy-start | bytes 100
  282.5 14.1 %copy-start.2 = (f32[8]{0:T(128)S(1)}, f32[8]{0:T(128)}, u32[]{:S(2)}) copy-start(f32[8]{0:T(128)} %param.11) | copy-start | bytes 100
  282.5 14.1 %copy-start.3 = (f32[2]{0:T(128)S(1)}, f32[2]{0:T(128)}, u32[]{:S(2)}) copy-start(f32[2]{0:T(128)} %param.13) | copy-start | bytes 28
  285.7 74.8 %all-to-all-start.1 = ((bf16[32,2,4096]{2,1,0:T(2,128)(2,1)}), bf16[32,2,4096]{2,1,0:T(2,128)(2,1)S(1)}, u32[]{:S(2)}, u32[]{:S(2)}) async-start(bf16[32,2,4096]{2,1,0:T(2,128)(2,1)} %reshape.89), calls=%async_computation.1 | async-start | bytes 1048576 | tf_op jit(solution)/shard_map/all_to_all | solution.py:27
  361.5 1.3 copy-start
Sparse Core Ops, SparseCore 0:
  68.4 83.2 all-gather.1
where the time goes:
time: 374 us; the launch traced here: 372 us
  waiting for transfers between devices  256 us (68%)
  local copies, waits for them, and re-layouts  53.6 us (14%)
  starting transfers between devices  39.7 us (11%)
  between operations  13.6 us (4%)
  matrix products  7.78 us (2%)
    all_to_all x1, waiting for transfers between devices, shards(): lax.all_to_all(amplitudes, 'row', split_axis=3, concat_axis=2, tiled=True)  192 us
    all_to_all x1, waiting for transfers between devices, shards(): lax.all_to_all(cycle_half, 'row', split_axis=2, concat_axis=3, tiled=True)  63.8 us
    unnamed x15, local copies, waits for them, and re-layouts  36.2 us
    all_to_all x1, starting transfers between devices, shards(): lax.all_to_all(amplitudes, 'row', split_axis=3, concat_axis=2, tiled=True)  29.3 us
    all_to_all x1, local copies, waits for them, and re-layouts, shards(): lax.all_to_all(amplitudes, 'row', split_axis=3, concat_axis=2, tiled=True)  12.8 us
    all_to_all x1, starting transfers between devices, shards(): lax.all_to_all(cycle_half, 'row', split_axis=2, concat_axis=3, tiled=True)  10.4 us
    dot_general x1, matrix products, contract(): jnp.einsum('iakc,kjcb->ijab', panel, amp_rows, preferred_element_type=jnp...  7.59 us
  transfers between devices with their start and end apart: 3, of which 2 were waited for; matrix products, arithmetic and copies ran while one was open for 5% of the time, Pallas kernels for 0%

commit v1 on v0

v1 whole, which is shorter than its diff:
```python
import functools

import jax
import jax.numpy as jnp
from jax import lax
from jax.experimental import pallas as pl
from jax.experimental.pallas import tpu as pltpu
from jax.sharding import PartitionSpec as P

TILE = 64
LANES = 128
ROWS = 32
NI = 8
NJ = 8
NK = 32
BV = 2048
NB = BV // TILE
KEEP_CAPS = (20, 24, 32)


def swap(v):
    return jnp.concatenate([v[..., TILE:], v[..., :TILE]], axis=-1)


def low_half(shape):
    return lax.broadcasted_iota(jnp.int32, shape, len(shape) - 1) < TILE


def list_kept(mask_ref, jt, idx_ref, pos_ref):
    if idx_ref is not None:
        for t in range(NB):
            idx_ref[t] = 0
    count = jnp.int32(0)
    for b in range(NB):
        if idx_ref is not None:
            idx_ref[count] = b
        if pos_ref is not None:
            pos_ref[b] = count
        count = count + jnp.minimum(mask_ref[jt, b], 1)


def pack_kernel(cap, mask_ref, jt_ref, x_ref, o_ref, xs_ref, idx_ref):
    full = cap // 8

    @pl.when(pl.program_id(0) == 0)
    def _():
        list_kept(mask_ref, jt_ref[0], idx_ref, None)

    xs_ref[...] = x_ref[:, 0].reshape(2 * NK, BV)

    def lanes_of(tile):
        return xs_ref[:, pl.ds(pl.multiple_of((tile // 2) * LANES, LANES), LANES)]

    def low(v, tile):
        return jnp.where(tile % 2 == 0, v, swap(v))

    def high(v, tile):
        return jnp.where(tile % 2 == 1, v, swap(v))

    for u in range(full):
        for q in range(4):
            t0 = idx_ref[8 * u + 2 * q]
            t1 = idx_ref[8 * u + 2 * q + 1]
            a = low(lanes_of(t0), t0)
            b = high(lanes_of(t1), t1)
            o_ref[q, 64 * u : 64 * u + 64, :] = jnp.concatenate([a[:, :TILE], b[:, TILE:]], axis=1)
    if cap % 8:
        for q in range(4):
            t0 = idx_ref[8 * full + q]
            v = lanes_of(t0)
            a = low(v[:32], t0)
            b = high(v[32:], t0)
            o_ref[q, 64 * full :, :] = jnp.concatenate([a[:, :TILE], b[:, TILE:]], axis=1)


def contract_kernel(cap, r_ref, w_ref, o_ref, x_ref):
    full = cap // 8
    for u in range(full):
        x_ref[:, LANES * u : LANES * (u + 1)] = r_ref[:, 64 * u : 64 * u + 64, :].reshape(ROWS * 64, LANES)
    if cap % 8:
        y = r_ref[:, 64 * full :, :]
        m = low_half(y.shape)
        z = jnp.zeros_like(y)
        both = jnp.concatenate([jnp.where(m, y, z), jnp.where(m, z, y)], axis=1)
        x_ref[:, LANES * full :] = both.reshape(ROWS * 64, LANES)
    p = jnp.dot(w_ref[...], x_ref[...], preferred_element_type=jnp.float32)
    for u in range(full):
        part = p[:, LANES * u : LANES * (u + 1)].reshape(ROWS, 16, LANES)
        o_ref[:, 16 * u : 16 * u + 16, :] = part.astype(jnp.bfloat16)
    if cap % 8:
        part = p[:, LANES * full :]
        part = (part + swap(part)).reshape(ROWS, 2, 8, LANES)
        folded = jnp.where(low_half((ROWS, 8, LANES)), part[:, 0], part[:, 1])
        o_ref[:, 16 * full :, :] = folded.astype(jnp.bfloat16)


def update_kernel(cap, mask_ref, jt_ref, c_ref, oth_ref, row_ref, vr_ref, o_ref, comp_ref, oths_ref, res_ref, pos_ref):
    full = cap // 8
    jt = jt_ref[0]

    @pl.when(pl.program_id(0) == 0)
    def _():
        list_kept(mask_ref, jt, None, pos_ref)

    oths_ref[...] = oth_ref[:, 0].reshape(16, BV).astype(jnp.float32)
    for u in range(full):
        for q in range(4):
            comp_ref[4 * u + q] = c_ref[q, 16 * u : 16 * u + 16, :].astype(jnp.float32)
    if cap % 8:
        m8 = low_half((8, LANES))
        for h in range(2):
            f0 = c_ref[2 * h, 16 * full :, :].astype(jnp.float32)
            f1 = c_ref[2 * h + 1, 16 * full :, :].astype(jnp.float32)
            comp_ref[4 * full + h, 0:8, :] = jnp.where(m8, f0, swap(f1))
            comp_ref[4 * full + h, 8:16, :] = jnp.where(m8, swap(f0), f1)
    m16 = low_half((16, LANES))
    row = row_ref[0]
    for lt in range(BV // LANES):
        sl = slice(LANES * lt, LANES * (lt + 1))
        p0 = jnp.minimum(pos_ref[2 * lt], cap - 1)
        p1 = jnp.minimum(pos_ref[2 * lt + 1], cap - 1)
        c0 = comp_ref[p0 // 2]
        c1 = comp_ref[p1 // 2]
        a = jnp.where(p0 % 2 == 0, c0, swap(c0))
        b = jnp.where(p1 % 2 == 1, c1, swap(c1))
        k0 = mask_ref[jt, 2 * lt].astype(jnp.float32)
        k1 = mask_ref[jt, 2 * lt + 1].astype(jnp.float32)
        keep = jnp.where(m16, k0, k1)
        cycle = jnp.where(m16, a, b)
        denominator = row - vr_ref[:, sl]
        res_ref[:, sl] = keep * (oths_ref[:, sl] + cycle) / denominator
    o_ref[...] = res_ref[...].reshape(NI, 2, BV).astype(jnp.bfloat16)[:, None]


def one_cap(cap, amplitudes, integrals, others, row_term, virtual_right, tile_mask, jt):
    full, half = divmod(cap, 8)
    half = int(half > 0)
    rows_in = 64 * full + 32 * half
    rows_out = 16 * full + 8 * half
    bf16 = jnp.bfloat16
    whole = pl.BlockSpec(memory_space=pltpu.VMEM)
    packed = pl.pallas_call(
        functools.partial(pack_kernel, cap),
        out_shape=jax.ShapeDtypeStruct((ROWS, rows_in, LANES), bf16),
        grid_spec=pltpu.PrefetchScalarGridSpec(
            num_scalar_prefetch=2,
            grid=(NJ,),
            in_specs=[pl.BlockSpec((NK, 1, 2, BV), lambda j, m, t: (0, j, 0, 0))],
            out_specs=pl.BlockSpec((4, rows_in, LANES), lambda j, m, t: (j, 0, 0)),
            scratch_shapes=[pltpu.VMEM((2 * NK, BV), bf16), pltpu.SMEM((NB,), jnp.int32)],
        ),
        name="pack",
    )(tile_mask, jt, amplitudes)
    received = lax.all_to_all(packed, "row", split_axis=0, concat_axis=0, tiled=True)

    own = integrals[:, :, 0, :].reshape(NI, ROWS, 2, TILE).transpose(3, 1, 0, 2).reshape(TILE, NI * TILE)
    gathered = lax.all_gather(own, "col", axis=0, tiled=False)
    by_row = gathered.reshape(NK, ROWS, 2, NI * TILE).transpose(1, 0, 2, 3).reshape(NK * TILE, NI * TILE)
    weights = by_row.T

    cycle = pl.pallas_call(
        functools.partial(contract_kernel, cap),
        out_shape=jax.ShapeDtypeStruct((ROWS, rows_out, LANES), bf16),
        in_specs=[whole, whole],
        out_specs=whole,
        scratch_shapes=[pltpu.VMEM((NK * TILE, LANES * (full + half)), bf16)],
        compiler_params=pltpu.CompilerParams(vmem_limit_bytes=40 << 20),
        name="contract",
    )(received, weights)
    returned = lax.all_to_all(cycle, "row", split_axis=0, concat_axis=0, tiled=True)

    return pl.pallas_call(
        functools.partial(update_kernel, cap),
        out_shape=jax.ShapeDtypeStruct(others.shape, bf16),
        grid_spec=pltpu.PrefetchScalarGridSpec(
            num_scalar_prefetch=2,
            grid=(NJ,),
            in_specs=[
                pl.BlockSpec((4, rows_out, LANES), lambda j, m, t: (j, 0, 0)),
                pl.BlockSpec((NI, 1, 2, BV), lambda j, m, t: (0, j, 0, 0)),
                pl.BlockSpec((1, 16, LANES), lambda j, m, t: (j, 0, 0)),
                pl.BlockSpec((1, BV), lambda j, m, t: (0, 0)),
            ],
            out_specs=pl.BlockSpec((NI, 1, 2, BV), lambda j, m, t: (0, j, 0, 0)),
            scratch_shapes=[
                pltpu.VMEM((cap // 2, 16, LANES), jnp.float32),
                pltpu.VMEM((16, BV), jnp.float32),
                pltpu.VMEM((16, BV), jnp.float32),
                pltpu.SMEM((NB,), jnp.int32),
            ],
        ),
        name="update",
    )(tile_mask, jt, returned, others, row_term, virtual_right[None])


def shards(
    amplitudes,
    integrals,
    others,
    occupied_left,
    occupied_right,
    virtual_left,
    virtual_right,
    tile_mask,
):
    jt = (lax.axis_index("col") * NJ // TILE).astype(jnp.int32).reshape(1)
    row_term = (
        occupied_left[None, :, None] + occupied_right[:, None, None] - virtual_left[None, None, :]
    ).reshape(NJ, NI * 2)
    row_term = jnp.broadcast_to(row_term[:, :, None], (NJ, NI * 2, LANES))
    most = jnp.max(jnp.sum(jnp.minimum(tile_mask, 1), axis=1))
    branch = jnp.sum((most > jnp.array(KEEP_CAPS[:-1], jnp.int32)).astype(jnp.int32))
    return lax.switch(
        branch,
        [functools.partial(one_cap, cap) for cap in KEEP_CAPS],
        amplitudes,
        integrals,
        others,
        row_term,
        virtual_right,
        tile_mask,
        jt,
    )


def solution(mesh):
    in_specs = (
        P(None, "col", "row", None),
        P(None, None, "col", None),
        P(None, "col", "row", None),
        P(),
        P("col"),
        P("row"),
        P(),
        P(),
    )
    out_specs = P(None, "col", "row", None)
    return jax.shard_map(shards, mesh=mesh, in_specs=in_specs, out_specs=out_specs, check_vma=False)
```

time: 374 us -> 247 us (0.66)
  waiting for transfers between devices: 256 us -> 161 us
  local copies, waits for them, and re-layouts: 53.6 us -> 13.4 us
  Pallas kernels: 0 us -> 14.5 us
  matrix products: 7.78 us -> 0 us
    all_to_all x2, waiting for transfers between devices: 255 us -> 75.7 us  [the longest x1 47.1 us: one_cap(): lax.all_to_all(cycle, 'row', split_axis=0, concat_axis=0, tiled=True)]
    all_gather x1, waiting for transfers between devices: 0.01 us -> 85.1 us  [one_cap(): gathered = lax.all_gather(own, 'col', axis=0, tiled=False)]
    unnamed x15 -> x2, local copies, waits for them, and re-layouts: 36.2 us -> 0.79 us
    pallas_call x0 -> x3, Pallas kernels: none -> 14.5 us  [the longest x1 6.96 us: one_cap(): pl.pallas_call(functools.partial(pack_kernel, cap), out_shape=jax.ShapeDt...]
    all_to_all x2 -> x0, local copies, waits for them, and re-layouts: 13 us -> none  [the longest x1 12.8 us: shards(): lax.all_to_all(amplitudes, 'row', split_axis=3, concat_axis=2, tiled=True)]
    dot_general x2 -> x0, matrix products: 7.78 us -> none  [the longest x1 7.59 us: contract(): jnp.einsum('iakc,kjcb->ijab', panel, amp_rows, preferred_element_type=jnp...]
    reshape x0 -> x3, local copies, waits for them, and re-layouts: none -> 5.9 us  [the longest x2 5.17 us: one_cap(): gathered.reshape(NK, ROWS, 2, NI * TILE).transpose(1, 0, 2, 3)]
    convert_element_type x4 -> x0, local copies, waits for them, and re-layouts: 4.27 us -> none  [the longest x1 1.65 us: shards(): cycle_half = cycle_term.astype(jnp.bfloat16)]
  transfers between devices with their start and end apart: 3 -> 3, of which waited for: 2 -> 3; matrix products, arithmetic and copies ran while one was open for 5% -> 5% of each run, Pallas kernels for 0% -> 0%
where the time goes in v1:
time: 247 us; the launch traced here: 246 us
  waiting for transfers between devices  161 us (65%)
  starting transfers between devices  39.7 us (16%)
  Pallas kernels  14.5 us (6%)
  between operations  14 us (6%)
  local copies, waits for them, and re-layouts  13.4 us (5%)
  other arithmetic  3.57 us (1%)
    all_gather x1, waiting for transfers between devices, one_cap(): gathered = lax.all_gather(own, 'col', axis=0, tiled=False)  85.1 us
    all_to_all x1, waiting for transfers between devices, one_cap(): lax.all_to_all(cycle, 'row', split_axis=0, concat_axis=0, tiled=True)  47.1 us
    all_to_all x1, starting transfers between devices, one_cap(): lax.all_to_all(packed, 'row', split_axis=0, concat_axis=0, tiled=True)  29.4 us
    all_to_all x1, waiting for transfers between devices, one_cap(): lax.all_to_all(packed, 'row', split_axis=0, concat_axis=0, tiled=True)  28.6 us
    all_to_all x1, starting transfers between devices, one_cap(): lax.all_to_all(cycle, 'row', split_axis=0, concat_axis=0, tiled=True)  10.2 us
    pallas_call x1, Pallas kernels, one_cap(): pl.pallas_call(functools.partial(pack_kernel, cap), out_shape=jax.ShapeDt...  6.96 us
    pallas_call x1, Pallas kernels, one_cap(): pl.pallas_call(functools.partial(update_kernel, cap), out_shape=jax.Shape...  6.04 us
    reshape x2, local copies, waits for them, and re-layouts, one_cap(): gathered.reshape(NK, ROWS, 2, NI * TILE).transpose(1, 0, 2, 3)  5.17 us
  transfers between devices with their start and end apart: 3, of which 3 were waited for; matrix products, arithmetic and copies ran while one was open for 5% of the time, Pallas kernels for 0%

profile of v1, /device:TPU:1, one launch (start us, length us, event | category | flops | bytes accessed | tf_op | source)
XLA Modules:
  0.0 246.4 jit_solution(6869966352216063672)
XLA Ops:
  6.5 0.8 minimum_reduce_fusion
  7.3 0.6 reduce_max.9
  8.0 2.0 fusion
  10.6 228.1 %conditional.1 = (bf16[8,8,2,2048]{3,2,1,0:T(2,128)(2,1)S(1)}) conditional(s32[]{:T(128)} %clamp.3, (s32[4,32]{1,0:T(4,128)}, s32[]{:T(128)}, bf16[32,8,2,2048]{3,2,1,0:T(2,128)(2,1)}, bf16[8,64,1,64]{3,1,2,0:T(8,128)(2,1)}, f32[2048]{0:T(1024)}, /*index=5*/bf16[8,8,2,2048]{3,2,1,0:T(2,128)(2,1)}, f32[8]{0:T(128)}, s32[]{:T(128)}, ...), branch_computations={%region_3.4_spmd, %region_4.5_spmd, %region_5.6_spmd} | conditional | flops 200 | bytes 44472864 | solution.py:213
  10.6 7.0 %pack.3 = bf16[32,160,128]{2,1,0:T(8,128)(2,1)} custom-call(s32[4,32]{1,0:T(4,128)} %get-tuple-element.50.mask_ref, s32[1]{0:T(128)} %bitcast.jt_ref, bf16[32,8,2,2048]{3,2,1,0:T(2,128)(2,1)} %get-tuple-element.100.x_ref), custom_call_target="tpu_custom_call" | custom-call | tf_op jit(solution)/shard_map/cond/branch_0_fun/pack/pallas_call | solution.py:142
  17.6 0.0 copy-start.7
  17.6 29.4 %all-to-all-start = ((bf16[32,160,128]{2,1,0:T(8,128)(2,1)}), bf16[32,160,128]{2,1,0:T(8,128)(2,1)S(1)}, u32[]{:S(2)}, u32[]{:S(2)}) async-start(bf16[32,160,128]{2,1,0:T(8,128)(2,1)} %pack.3), calls=%async_computation | async-start | bytes 2621440 | tf_op jit(solution)/shard_map/cond/branch_0_fun/all_to_all | solution.py:154
  47.0 0.0 all-gather.4.cloned.1.call-start
  47.1 0.0 copy-done.7
  47.1 0.1 copy.76
  47.2 0.1 copy.58
  47.3 0.7 copy.59
  48.0 0.0 all-gather.4.cloned.1.call-update
  48.0 85.1 %all-gather.4.cloned.1.call-done = bf16[32,64,512]{2,1,0:T(8,128)(2,1)} async-done(((bf16[1,64,512]{2,1,0:T(8,128)(2,1)}), bf16[32,64,512]{2,1,0:T(8,128)(2,1)}) %all-gather.4.cloned.1.call-update) | async-done | bytes 2097168 | tf_op jit(solution)/shard_map/cond/branch_0_fun/all_gather | solution.py:157
  133.2 2.8 %copy.60 = bf16[32,64,512]{2,0,1:T(8,128)(2,1)S(1)} copy(bf16[32,64,512]{2,1,0:T(8,128)(2,1)} %all-gather.4.cloned.1.call-done) | data formatting | bytes 4194304 | tf_op jit(solution)/shard_map/cond/branch_0_fun/all_gather | solution.py:157
  135.9 2.2 copy.61
  138.1 2.2 reshape.69
  140.3 2.9 %copy.62 = bf16[2048,512]{0,1:T(8,128)(2,1)S(1)} copy(bf16[2048,512]{1,0:T(8,128)(2,1)} %reshape.69) | data formatting | bytes 4194304 | tf_op jit(solution)/shard_map/cond/branch_0_fun/reshape | solution.py:158
  143.3 28.6 %all-to-all-done.r_ref = bf16[32,160,128]{2,1,0:T(8,128)(2,1)S(1)} async-done(((bf16[32,160,128]{2,1,0:T(8,128)(2,1)}), bf16[32,160,128]{2,1,0:T(8,128)(2,1)S(1)}, u32[]{:S(2)}, u32[]{:S(2)}) %all-to-all-start) | async-done | bytes 1310752 | tf_op jit(solution)/shard_map/cond/branch_0_fun/all_to_all | solution.py:154
  171.9 0.0 copy-start.20
  171.9 0.0 copy-start.17
  171.9 0.0 copy-start.23
  171.9 0.0 copy-start.11
  171.9 0.0 copy-start.14
  171.9 1.5 contract.3
  173.4 0.0 copy-start.1
  173.4 0.7 copy-done.1
  174.1 10.2 %all-to-all-start.1 = ((bf16[32,40,128]{2,1,0:T(8,128)(2,1)}), bf16[32,40,128]{2,1,0:T(8,128)(2,1)S(1)}, u32[]{:S(2)}, u32[]{:S(2)}) async-start(bf16[32,40,128]{2,1,0:T(8,128)(2,1)} %copy-done.1), calls=%async_computation.1 | async-start | bytes 655360 | tf_op jit(solution)/shard_map/cond/branch_0_fun/all_to_all | solution.py:170
  184.3 0.0 copy-done.20
  184.4 0.1 sub.49
  184.4 0.0 copy-done.17
  184.4 0.0 copy-done.23
  184.4 0.1 broadcast_add_fusion
  184.5 0.1 broadcast_subtract_fusion
  184.6 0.1 copy.63
  184.7 47.1 %all-to-all-done.1.c_ref = bf16[32,40,128]{2,1,0:T(8,128)(2,1)S(1)} async-done(((bf16[32,40,128]{2,1,0:T(8,128)(2,1)}), bf16[32,40,128]{2,1,0:T(8,128)(2,1)S(1)}, u32[]{:S(2)}, u32[]{:S(2)}) %all-to-all-start.1) | async-done | bytes 327712 | tf_op jit(solution)/shard_map/cond/branch_0_fun/all_to_all | solution.py:170
  231.7 0.0 copy-start.6
  231.7 0.7 broadcast_in_dim.18.row_ref
  232.4 0.0 copy-done.6
  232.4 0.0 copy-done.11
  232.4 0.0 copy-done.14
  232.4 6.0 %update.3 = bf16[8,8,2,2048]{3,2,1,0:T(2,128)(2,1)S(1)} custom-call(s32[4,32]{1,0:T(4,128)S(1)} %copy-done.11, s32[1]{0:T(128)} %bitcast.jt_ref, bf16[32,40,128]{2,1,0:T(8,128)(2,1)} %copy-done.6, bf16[8,8,2,2048]{3,2,1,0:T(2,128)(2,1)} %get-tuple-element.109.oth_ref, f32[8,16,128]{2,1,0:T(8,128)} %broadcast_in_dim.18.row_ref, f32[1,2048]{1,0:T(1,128)S(1)} %bitcast.45), custom_call_target="tpu_custom_call" | custom-call | tf_op jit(solution)/shard_map/cond/branch_0_fun/update/pallas_call | solution.py:172
  238.7 0.0 copy-start.10
  238.7 0.8 copy-done.10
  (2 shorter events, 0.0 us)
Async XLA Ops:
  17.6 29.5 %copy-start.7 = (bf16[8,64,1,64]{3,1,2,0:T(8,128)(2,1)S(1)}, bf16[8,64,1,64]{3,1,2,0:T(8,128)(2,1)}, u32[]{:S(2)}) copy-start(bf16[8,64,1,64]{3,1,2,0:T(8,128)(2,1)} %get-tuple-element.307) | copy-start | bytes 196612 | tf_op jit(solution)/shard_map/cond
  17.6 154.3 %all-to-all-start = ((bf16[32,160,128]{2,1,0:T(8,128)(2,1)}), bf16[32,160,128]{2,1,0:T(8,128)(2,1)S(1)}, u32[]{:S(2)}, u32[]{:S(2)}) async-start(bf16[32,160,128]{2,1,0:T(8,128)(2,1)} %pack.3), calls=%async_computation | async-start | bytes 2621440 | tf_op jit(solution)/shard_map/cond/branch_0_fun/all_to_all | solution.py:154
  47.0 86.1 %all-gather.4.cloned.1.call-start = ((), (), s32[]{:S(2)}) async-start(), calls=%async_computation.6 | async-start | bytes 2162688 | tf_op jit(solution)/shard_map/cond/branch_0_fun/all_gather | solution.py:157
  171.9 12.5 %copy-start.20 = (f32[2]{0:T(128)S(1)}, f32[2]{0:T(128)}, u32[]{:S(2)}) copy-start(f32[2]{0:T(128)} %get-tuple-element.193) | copy-start | bytes 28 | tf_op jit(solution)/shard_map/cond
  171.9 12.6 %copy-start.17 = (f32[8]{0:T(128)S(1)}, f32[8]{0:T(128)}, u32[]{:S(2)}) copy-start(f32[8]{0:T(128)} %get-tuple-element.196) | copy-start | bytes 100 | tf_op jit(solution)/shard_map/cond
  171.9 12.6 %copy-start.23 = (f32[8]{0:T(128)S(1)}, f32[8]{0:T(128)}, u32[]{:S(2)}) copy-start(f32[8]{0:T(128)} %get-tuple-element.199) | copy-start | bytes 100 | tf_op jit(solution)/shard_map/cond
  171.9 60.6 %copy-start.11 = (s32[4,32]{1,0:T(4,128)S(1)}, s32[4,32]{1,0:T(4,128)}, u32[]{:S(2)}) copy-start(s32[4,32]{1,0:T(4,128)} %get-tuple-element.50.mask_ref) | copy-start | bytes 1540 | tf_op jit(solution)/shard_map/cond
  171.9 60.6 %copy-start.14 = (f32[2048]{0:T(1024)S(1)}, f32[2048]{0:T(1024)}, u32[]{:S(2)}) copy-start(f32[2048]{0:T(1024)} %get-tuple-element.106) | copy-start | bytes 24580 | tf_op jit(solution)/shard_map/cond
  173.4 0.7 copy-start.1
  174.1 57.6 %all-to-all-start.1 = ((bf16[32,40,128]{2,1,0:T(8,128)(2,1)}), bf16[32,40,128]{2,1,0:T(8,128)(2,1)S(1)}, u32[]{:S(2)}, u32[]{:S(2)}) async-start(bf16[32,40,128]{2,1,0:T(8,128)(2,1)} %copy-done.1), calls=%async_computation.1 | async-start | bytes 655360 | tf_op jit(solution)/shard_map/cond/branch_0_fun/all_to_all | solution.py:170
  231.7 0.7 copy-start.6
  238.7 0.8 copy-start.10
Sparse Core Ops, SparseCore 0:
  52.1 80.9 all-gather.3

commit v2 on v0

v2 whole, which is shorter than its diff:
```python
import functools

import jax
import jax.numpy as jnp
from jax import lax
from jax.experimental import pallas as pl
from jax.experimental.pallas import tpu as pltpu
from jax.sharding import PartitionSpec as P

TILE = 64
LANES = 128
ROWS = 32
NI = 8
NJ = 8
NK = 32
BV = 2048
NB = BV // TILE
KEEP_CAPS = (18, 20, 24)


def turn(v, by):
    by %= LANES
    return v if by == 0 else jnp.concatenate([v[..., LANES - by :], v[..., : LANES - by]], axis=-1)


def lane_group(shape, width):
    return lax.broadcasted_iota(jnp.int32, shape, len(shape) - 1) // width


def pieces(cap):
    found = []
    tile, row_in, row_out = 0, 0, 0
    for step, fold in [(8, 1)] * (cap // 8) + [(4, 2)] * (cap % 8 // 4) + [(2, 4)] * (cap % 4 // 2):
        found.append((tile, fold, row_in, row_out))
        tile, row_in, row_out = tile + step, row_in + 64 // fold, row_out + 16 // fold
    return found, row_in, row_out


def list_kept(mask_ref, jt, idx_ref, pos_ref):
    if idx_ref is not None:
        for t in range(2 * NB):
            idx_ref[t] = 0
    count = jnp.int32(0)
    for b in range(NB):
        if idx_ref is not None:
            idx_ref[count] = b
        if pos_ref is not None:
            pos_ref[b] = count
        count = count + jnp.minimum(mask_ref[jt, b], 1)


def pack_kernel(cap, mask_ref, jt_ref, x_ref, o_ref, xs_ref, idx_ref):
    @pl.when(pl.program_id(0) == 0)
    def _():
        list_kept(mask_ref, jt_ref[0], idx_ref, None)

    xs_ref[...] = x_ref[:, 0].reshape(2 * NK, BV)

    def lanes_of(tile):
        return xs_ref[:, pl.ds(pl.multiple_of((tile // 2) * LANES, LANES), LANES)]

    def low(v, tile):
        return jnp.where(tile % 2 == 0, v, turn(v, TILE))

    def high(v, tile):
        return jnp.where(tile % 2 == 1, v, turn(v, TILE))

    first = jt_ref[1]
    for tile, fold, row, _ in pieces(cap)[0]:
        for q in range(4):
            if fold == 1:
                t0 = idx_ref[first + tile + 2 * q]
                t1 = idx_ref[first + tile + 2 * q + 1]
                parts = [low(lanes_of(t0), t0)[:, :TILE], high(lanes_of(t1), t1)[:, TILE:]]
            elif fold == 2:
                t0 = idx_ref[first + tile + q]
                v = lanes_of(t0)
                parts = [low(v[:32], t0)[:, :TILE], high(v[32:], t0)[:, TILE:]]
            else:
                t0 = idx_ref[first + tile + q // 2]
                v = low(lanes_of(t0), t0)
                parts = [turn(v[16 * g : 16 * g + 16], 32 * (g - q % 2))[:, 32 * g : 32 * g + 32] for g in range(4)]
            o_ref[q, row : row + 64 // fold, :] = jnp.concatenate(parts, axis=1)


def contract_kernel(cap, r_ref, w_ref, o_ref, x_ref):
    found = pieces(cap)[0]
    for n, (_, fold, row, _) in enumerate(found):
        y = r_ref[:, row : row + 64 // fold, :]
        if fold > 1:
            group = lane_group(y.shape, LANES // fold)
            y = jnp.concatenate([jnp.where(group == g, y, jnp.zeros_like(y)) for g in range(fold)], axis=1)
        x_ref[:, LANES * n : LANES * (n + 1)] = y.reshape(ROWS * 64, LANES)
    p = jnp.dot(w_ref[...], x_ref[...], preferred_element_type=jnp.float32)
    for n, (_, fold, _, row) in enumerate(found):
        part = p[:, LANES * n : LANES * (n + 1)]
        if fold > 1:
            part = part + turn(part, 64)
        if fold > 2:
            part = part + turn(part, 32)
        height = 16 // fold
        part = part.reshape(ROWS, 16, LANES)
        out = part[:, :height]
        group = lane_group(out.shape, LANES // fold)
        for g in range(1, fold):
            out = jnp.where(group == g, part[:, height * g : height * (g + 1)], out)
        o_ref[:, row : row + height, :] = out.astype(jnp.bfloat16)


def prepare_kernel(mask_ref, jt_ref, oth_ref, row_ref, vr_ref, oths_ref, factor_ref):
    jt = jt_ref[0]
    low = lane_group((16, LANES), TILE) == 0

    def one_j(j, carry):
        oths_ref[j] = oth_ref[:, j].reshape(16, BV)
        row = row_ref[j]
        for lt in range(BV // LANES):
            sl = slice(LANES * lt, LANES * (lt + 1))
            k0 = mask_ref[jt, 2 * lt].astype(jnp.float32)
            k1 = mask_ref[jt, 2 * lt + 1].astype(jnp.float32)
            factor_ref[j, :, sl] = jnp.where(low, k0, k1) / (row - vr_ref[:, sl])
        return carry

    lax.fori_loop(0, NJ, one_j, 0)


def update_kernel(cap, repeated, mask_ref, jt_ref, c_ref, oths_ref, factor_ref, *refs):
    if repeated:
        before_ref, *refs = refs
    o_ref, comp_ref, res_ref, pos_ref = refs
    first = jt_ref[1]
    found = pieces(cap)[0]
    list_kept(mask_ref, jt_ref[0], None, pos_ref)
    low = lane_group((16, LANES), TILE) == 0

    def one_j(j, carry):
        for tile, fold, _, row in found:
            blocks = [c_ref[4 * j + q, row : row + 16 // fold, :].astype(jnp.float32) for q in range(4)]
            if fold == 1:
                for q in range(4):
                    comp_ref[tile // 2 + q] = blocks[q]
            elif fold == 2:
                m = lane_group((8, LANES), TILE) == 0
                for h in range(2):
                    f0, f1 = blocks[2 * h], blocks[2 * h + 1]
                    comp_ref[tile // 2 + h, 0:8, :] = jnp.where(m, f0, turn(f1, TILE))
                    comp_ref[tile // 2 + h, 8:16, :] = jnp.where(m, turn(f0, TILE), f1)
            else:
                group = lane_group((4, LANES), 32)
                for g in range(4):
                    out = turn(blocks[0], -32 * g)
                    for q in range(1, 4):
                        out = jnp.where(group == q, turn(blocks[q], 32 * (q - g)), out)
                    comp_ref[tile // 2, 4 * g : 4 * g + 4, :] = out
        for lt in range(BV // LANES):
            sl = slice(LANES * lt, LANES * (lt + 1))
            p0 = jnp.clip(pos_ref[2 * lt] - first, 0, cap - 1)
            p1 = jnp.clip(pos_ref[2 * lt + 1] - first, 0, cap - 1)
            a = pltpu.roll(comp_ref[p0 // 2], TILE * (p0 % 2), 1)
            b = pltpu.roll(comp_ref[p1 // 2], TILE * (1 - p1 % 2), 1)
            cycle = jnp.where(low, a, b)
            res_ref[:, sl] = factor_ref[j, :, sl] * (oths_ref[j, :, sl].astype(jnp.float32) + cycle)
        if repeated:
            done = before_ref[:, j].reshape(16, BV).astype(jnp.float32)
            for lt in range(BV // LANES):
                sl = slice(LANES * lt, LANES * (lt + 1))
                d0 = (pos_ref[2 * lt] < first).astype(jnp.int32)
                d1 = (pos_ref[2 * lt + 1] < first).astype(jnp.int32)
                res_ref[:, sl] = jnp.where(jnp.where(low, d0, d1) > 0, done[:, sl], res_ref[:, sl])
        o_ref[:, j] = res_ref[...].reshape(NI, 2, BV).astype(jnp.bfloat16)
        return carry

    lax.fori_loop(0, NJ, one_j, 0)


def one_pass(cap, before, amplitudes, integrals, others, row_term, virtual_right, tile_mask, jt):
    found, rows_in, rows_out = pieces(cap)
    bf16 = jnp.bfloat16
    whole = pl.BlockSpec(memory_space=pltpu.VMEM)
    scalars = pl.BlockSpec(memory_space=pltpu.SMEM)
    packed = pl.pallas_call(
        functools.partial(pack_kernel, cap),
        out_shape=jax.ShapeDtypeStruct((ROWS, rows_in, LANES), bf16),
        grid_spec=pltpu.PrefetchScalarGridSpec(
            num_scalar_prefetch=2,
            grid=(NJ,),
            in_specs=[pl.BlockSpec((NK, 1, 2, BV), lambda j, m, t: (0, j, 0, 0))],
            out_specs=pl.BlockSpec((4, rows_in, LANES), lambda j, m, t: (j, 0, 0)),
            scratch_shapes=[pltpu.VMEM((2 * NK, BV), bf16), pltpu.SMEM((2 * NB,), jnp.int32)],
        ),
        name="pack",
    )(tile_mask, jt, amplitudes)
    received = lax.all_to_all(packed, "row", split_axis=0, concat_axis=0, tiled=True)

    own = integrals[:, :, 0, :].reshape(NI, ROWS, 2, TILE).transpose(3, 1, 0, 2).reshape(TILE, NI * TILE)
    gathered = lax.all_gather(own, "col", axis=0, tiled=False)
    by_row = gathered.reshape(NK, ROWS, 2, NI * TILE).transpose(1, 0, 2, 3).reshape(NK * TILE, NI * TILE)
    weights = by_row.T

    cycle = pl.pallas_call(
        functools.partial(contract_kernel, cap),
        out_shape=jax.ShapeDtypeStruct((ROWS, rows_out, LANES), bf16),
        in_specs=[whole, whole],
        out_specs=whole,
        scratch_shapes=[
            pltpu.VMEM((NK * TILE, LANES * len(found)), bf16),
        ],
        compiler_params=pltpu.CompilerParams(vmem_limit_bytes=40 << 20),
        name="contract",
    )(received, weights)
    returned = lax.all_to_all(cycle, "row", split_axis=0, concat_axis=0, tiled=True)

    residual, factor = pl.pallas_call(
        prepare_kernel,
        out_shape=[
            jax.ShapeDtypeStruct((NJ, 2 * NI, BV), bf16),
            jax.ShapeDtypeStruct((NJ, 2 * NI, BV), jnp.float32),
        ],
        in_specs=[scalars, scalars, whole, whole, whole],
        out_specs=[whole, whole],
        compiler_params=pltpu.CompilerParams(vmem_limit_bytes=40 << 20),
        name="prepare",
    )(tile_mask, jt, others, row_term, virtual_right[None])

    return pl.pallas_call(
        functools.partial(update_kernel, cap, bool(before)),
        out_shape=jax.ShapeDtypeStruct(others.shape, bf16),
        in_specs=[scalars, scalars, whole, whole, whole] + [whole] * len(before),
        out_specs=whole,
        scratch_shapes=[
            pltpu.VMEM((cap // 2, 16, LANES), jnp.float32),
            pltpu.VMEM((16, BV), jnp.float32),
            pltpu.SMEM((NB,), jnp.int32),
        ],
        compiler_params=pltpu.CompilerParams(vmem_limit_bytes=40 << 20),
        name="update",
    )(tile_mask, jt, returned, residual, factor, *before)


def once(cap, most, jt, *arrays):
    return one_pass(cap, [], *arrays, jnp.stack([jt, jnp.int32(0)]))


def repeatedly(cap, most, jt, *arrays):
    def step(n, before):
        return one_pass(cap, [before], *arrays, jnp.stack([jt, n * cap]))

    passes = jnp.maximum((most + cap - 1) // cap, 1)
    return lax.fori_loop(0, passes, step, jnp.zeros_like(arrays[2]))


def shards(
    amplitudes,
    integrals,
    others,
    occupied_left,
    occupied_right,
    virtual_left,
    virtual_right,
    tile_mask,
):
    jt = (lax.axis_index("col") // (TILE // NJ)).astype(jnp.int32)
    row_term = (
        occupied_left[None, :, None] + occupied_right[:, None, None] - virtual_left[None, None, :]
    ).reshape(NJ, NI * 2)
    row_term = jnp.broadcast_to(row_term[:, :, None], (NJ, NI * 2, LANES))
    most = jnp.max(jnp.sum(tile_mask, axis=1))
    branch = sum((most > cap).astype(jnp.int32) for cap in KEEP_CAPS[:-1])
    steps = [functools.partial(once, cap) for cap in KEEP_CAPS[:-1]] + [functools.partial(repeatedly, KEEP_CAPS[-1])]
    return lax.switch(
        branch, steps, most, jt, amplitudes, integrals, others, row_term, virtual_right, tile_mask
    )


def solution(mesh):
    in_specs = (
        P(None, "col", "row", None),
        P(None, None, "col", None),
        P(None, "col", "row", None),
        P(),
        P("col"),
        P("row"),
        P(),
        P(),
    )
    out_specs = P(None, "col", "row", None)
    return jax.shard_map(shards, mesh=mesh, in_specs=in_specs, out_specs=out_specs, check_vma=False)
```

time: 374 us -> 244 us (0.65)
  waiting for transfers between devices: 256 us -> 160 us
  local copies, waits for them, and re-layouts: 53.6 us -> 12.6 us
  Pallas kernels: 0 us -> 13.6 us
  matrix products: 7.78 us -> 0 us
    all_to_all x2, waiting for transfers between devices: 255 us -> 74.6 us  [the longest x1 46 us: one_pass(): lax.all_to_all(cycle, 'row', split_axis=0, concat_axis=0, tiled=True)]
    all_gather x1, waiting for transfers between devices: 0.01 us -> 84.9 us  [one_pass(): gathered = lax.all_gather(own, 'col', axis=0, tiled=False)]
    unnamed x15 -> x0, local copies, waits for them, and re-layouts: 36.2 us -> none
    pallas_call x0 -> x4, Pallas kernels: none -> 13.6 us  [the longest x1 6.98 us: one_pass(): pl.pallas_call(functools.partial(pack_kernel, cap), out_shape=jax.ShapeDt...]
    all_to_all x2 -> x0, local copies, waits for them, and re-layouts: 13 us -> none  [the longest x1 12.8 us: shards(): lax.all_to_all(amplitudes, 'row', split_axis=3, concat_axis=2, tiled=True)]
    dot_general x2 -> x0, matrix products: 7.78 us -> none  [the longest x1 7.59 us: contract(): jnp.einsum('iakc,kjcb->ijab', panel, amp_rows, preferred_element_type=jnp...]
    reshape x0 -> x3, local copies, waits for them, and re-layouts: none -> 5.88 us  [the longest x2 5.15 us: one_pass(): gathered.reshape(NK, ROWS, 2, NI * TILE).transpose(1, 0, 2, 3)]
    convert_element_type x4 -> x0, local copies, waits for them, and re-layouts: 4.27 us -> none  [the longest x1 1.65 us: shards(): cycle_half = cycle_term.astype(jnp.bfloat16)]
  transfers between devices with their start and end apart: 3 -> 3, of which waited for: 2 -> 3; matrix products, arithmetic and copies ran while one was open for 5% -> 5% of each run, Pallas kernels for 0% -> 1%
where the time goes in v2:
time: 244 us; the launch traced here: 243 us
  waiting for transfers between devices  160 us (66%)
  starting transfers between devices  39.9 us (16%)
  between operations  14.5 us (6%)
  Pallas kernels  13.6 us (6%)
  local copies, waits for them, and re-layouts  12.6 us (5%)
  other arithmetic  2.91 us (1%)
    all_gather x1, waiting for transfers between devices, one_pass(): gathered = lax.all_gather(own, 'col', axis=0, tiled=False)  84.9 us
    all_to_all x1, waiting for transfers between devices, one_pass(): lax.all_to_all(cycle, 'row', split_axis=0, concat_axis=0, tiled=True)  46 us
    all_to_all x1, starting transfers between devices, one_pass(): lax.all_to_all(packed, 'row', split_axis=0, concat_axis=0, tiled=True)  29.4 us
    all_to_all x1, waiting for transfers between devices, one_pass(): lax.all_to_all(packed, 'row', split_axis=0, concat_axis=0, tiled=True)  28.6 us
    all_to_all x1, starting transfers between devices, one_pass(): lax.all_to_all(cycle, 'row', split_axis=0, concat_axis=0, tiled=True)  10.2 us
    pallas_call x1, Pallas kernels, one_pass(): pl.pallas_call(functools.partial(pack_kernel, cap), out_shape=jax.ShapeDt...  6.98 us
    reshape x2, local copies, waits for them, and re-layouts, one_pass(): gathered.reshape(NK, ROWS, 2, NI * TILE).transpose(1, 0, 2, 3)  5.15 us
  transfers between devices with their start and end apart: 3, of which 3 were waited for; matrix products, arithmetic and copies ran while one was open for 5% of the time, Pallas kernels for 1%

profile of v2, /device:TPU:1, one launch (start us, length us, event | category | flops | bytes accessed | tf_op | source)
XLA Modules:
  0.0 243.3 jit_solution(14630207101549203440)
XLA Ops:
  6.5 0.8 reduce_sum.9
  7.3 0.6 reduce_max.9
  9.1 0.7 broadcast_add_fusion
  9.9 0.7 sub.36
  10.5 0.1 sub.37
  10.6 0.1 broadcast_subtract_fusion
  10.7 0.1 copy.47
  10.8 0.1 broadcast_in_dim.10
  10.9 225.6 %conditional.1 = (bf16[8,8,2,2048]{3,2,1,0:T(2,128)(2,1)}) conditional(s32[]{:T(128)} %clamp.3, (s32[]{:T(128)}, s32[4,32]{1,0:T(4,128)}, bf16[32,8,2,2048]{3,2,1,0:T(2,128)(2,1)}, bf16[8,64,1,64]{3,1,2,0:T(8,128)(2,1)}, f32[2048]{0:T(1024)}, /*index=5*/bf16[8,8,2,2048]{3,2,1,0:T(2,128)(2,1)}, ...), branch_computations={%region_2.3_spmd, %region_3.4_spmd, %region_4.7_spmd} | conditional | flops 15 | bytes 33262176 | solution.py:270
  10.9 0.7 pad_add_fusion.1.jt_ref
  11.5 7.0 %pack.4 = bf16[32,160,128]{2,1,0:T(8,128)(2,1)} custom-call(s32[4,32]{1,0:T(4,128)} %get-tuple-element.102.mask_ref, s32[2]{0:T(128)} %pad_add_fusion.1.jt_ref, bf16[32,8,2,2048]{3,2,1,0:T(2,128)(2,1)} %get-tuple-element.104.x_ref), custom_call_target="tpu_custom_call" | custom-call | tf_op jit(solution)/shard_map/cond/branch_1_fun/pack/pallas_call | solution.py:181
  18.5 0.0 copy-start.7
  18.5 29.4 %all-to-all-start.2 = ((bf16[32,160,128]{2,1,0:T(8,128)(2,1)}), bf16[32,160,128]{2,1,0:T(8,128)(2,1)S(1)}, u32[]{:S(2)}, u32[]{:S(2)}) async-start(bf16[32,160,128]{2,1,0:T(8,128)(2,1)} %pack.4), calls=%async_computation.2 | async-start | bytes 2621440 | tf_op jit(solution)/shard_map/cond/branch_1_fun/all_to_all | solution.py:193
  47.9 0.2 all-gather.6.cloned.1.call-start
  48.1 0.0 copy-done.7
  48.1 0.1 copy.49
  48.2 0.1 copy.37
  48.4 0.7 copy.38
  49.1 0.0 all-gather.6.cloned.1.call-update
  49.1 84.9 %all-gather.6.cloned.1.call-done = bf16[32,64,512]{2,1,0:T(8,128)(2,1)} async-done(((bf16[1,64,512]{2,1,0:T(8,128)(2,1)}), bf16[32,64,512]{2,1,0:T(8,128)(2,1)}) %all-gather.6.cloned.1.call-update) | async-done | bytes 2097168 | tf_op jit(solution)/shard_map/cond/branch_1_fun/all_gather | solution.py:196
  134.1 2.8 %copy.39 = bf16[32,64,512]{2,0,1:T(8,128)(2,1)S(1)} copy(bf16[32,64,512]{2,1,0:T(8,128)(2,1)} %all-gather.6.cloned.1.call-done) | data formatting | bytes 4194304 | tf_op jit(solution)/shard_map/cond/branch_1_fun/all_gather | solution.py:196
  136.8 2.2 copy.40
  139.0 2.2 reshape.70
  141.2 2.9 %copy.41 = bf16[2048,512]{0,1:T(8,128)(2,1)S(1)} copy(bf16[2048,512]{1,0:T(8,128)(2,1)} %reshape.70) | data formatting | bytes 4194304 | tf_op jit(solution)/shard_map/cond/branch_1_fun/reshape | solution.py:197
  144.1 28.6 %all-to-all-done.2.r_ref = bf16[32,160,128]{2,1,0:T(8,128)(2,1)S(1)} async-done(((bf16[32,160,128]{2,1,0:T(8,128)(2,1)}), bf16[32,160,128]{2,1,0:T(8,128)(2,1)S(1)}, u32[]{:S(2)}, u32[]{:S(2)}) %all-to-all-start.2) | async-done | bytes 1310752 | tf_op jit(solution)/shard_map/cond/branch_1_fun/all_to_all | solution.py:193
  172.8 0.0 copy-start.4
  172.8 0.0 copy-start.9
  172.8 0.0 copy-start.12
  172.8 1.5 contract.4
  174.3 0.0 copy-start
  174.3 0.7 copy-done
  175.0 10.2 %all-to-all-start.3 = ((bf16[32,40,128]{2,1,0:T(8,128)(2,1)}), bf16[32,40,128]{2,1,0:T(8,128)(2,1)S(1)}, u32[]{:S(2)}, u32[]{:S(2)}) async-start(bf16[32,40,128]{2,1,0:T(8,128)(2,1)} %copy-done), calls=%async_computation.3 | async-start | bytes 655360 | tf_op jit(solution)/shard_map/cond/branch_1_fun/all_to_all | solution.py:211
  185.2 0.0 copy-done.4
  185.2 0.0 copy-done.9
  185.3 0.0 copy-done.12
  185.3 1.3 prepare.4
  186.6 46.0 %all-to-all-done.3.c_ref = bf16[32,40,128]{2,1,0:T(8,128)(2,1)S(1)} async-done(((bf16[32,40,128]{2,1,0:T(8,128)(2,1)}), bf16[32,40,128]{2,1,0:T(8,128)(2,1)S(1)}, u32[]{:S(2)}, u32[]{:S(2)}) %all-to-all-start.3) | async-done | bytes 327712 | tf_op jit(solution)/shard_map/cond/branch_1_fun/all_to_all | solution.py:211
  232.6 3.8 %update.4 = bf16[8,8,2,2048]{3,2,1,0:T(2,128)(2,1)} custom-call(s32[4,32]{1,0:T(4,128)S(1)} %copy-done.9, s32[2]{0:T(128)S(1)} %copy-done.4, bf16[32,40,128]{2,1,0:T(8,128)(2,1)S(1)} %all-to-all-done.3.c_ref, bf16[8,16,2048]{2,1,0:T(8,128)(2,1)S(1)} %get-tuple-element.109.oths_ref, f32[8,16,2048]{2,1,0:T(8,128)S(1)} %get-tuple-element.110.factor_ref), custom_call_target="tpu_custom_call" | custom-call | tf_op jit(solution)/shard_map/cond/branch_1_fun/update/pallas_call | solution.py:225
  (1 shorter events, 0.0 us)
Async XLA Ops:
  18.5 29.7 %copy-start.7 = (bf16[8,64,1,64]{3,1,2,0:T(8,128)(2,1)S(1)}, bf16[8,64,1,64]{3,1,2,0:T(8,128)(2,1)}, u32[]{:S(2)}) copy-start(bf16[8,64,1,64]{3,1,2,0:T(8,128)(2,1)} %get-tuple-element.189) | copy-start | bytes 196612 | tf_op jit(solution)/shard_map/cond
  18.5 154.3 %all-to-all-start.2 = ((bf16[32,160,128]{2,1,0:T(8,128)(2,1)}), bf16[32,160,128]{2,1,0:T(8,128)(2,1)S(1)}, u32[]{:S(2)}, u32[]{:S(2)}) async-start(bf16[32,160,128]{2,1,0:T(8,128)(2,1)} %pack.4), calls=%async_computation.2 | async-start | bytes 2621440 | tf_op jit(solution)/shard_map/cond/branch_1_fun/all_to_all | solution.py:193
  47.9 86.1 %all-gather.6.cloned.1.call-start = ((), (), s32[]{:S(2)}) async-start(), calls=%async_computation.7 | async-start | bytes 2162688 | tf_op jit(solution)/shard_map/cond/branch_1_fun/all_gather | solution.py:196
  172.8 12.5 %copy-start.4 = (s32[2]{0:T(128)S(1)}, s32[2]{0:T(128)}, u32[]{:S(2)}) copy-start(s32[2]{0:T(128)} %pad_add_fusion.1.jt_ref) | copy-start | bytes 28 | tf_op jit(solution)/shard_map/cond
  172.8 12.5 %copy-start.9 = (s32[4,32]{1,0:T(4,128)S(1)}, s32[4,32]{1,0:T(4,128)}, u32[]{:S(2)}) copy-start(s32[4,32]{1,0:T(4,128)} %get-tuple-element.102.mask_ref) | copy-start | bytes 1540 | tf_op jit(solution)/shard_map/cond
  172.8 12.5 %copy-start.12 = (f32[2048]{0:T(1024)S(1)}, f32[2048]{0:T(1024)}, u32[]{:S(2)}) copy-start(f32[2048]{0:T(1024)} %get-tuple-element.108) | copy-start | bytes 24580 | tf_op jit(solution)/shard_map/cond
  174.3 0.7 copy-start
  175.0 57.6 %all-to-all-start.3 = ((bf16[32,40,128]{2,1,0:T(8,128)(2,1)}), bf16[32,40,128]{2,1,0:T(8,128)(2,1)S(1)}, u32[]{:S(2)}, u32[]{:S(2)}) async-start(bf16[32,40,128]{2,1,0:T(8,128)(2,1)} %copy-done), calls=%async_computation.3 | async-start | bytes 655360 | tf_op jit(solution)/shard_map/cond/branch_1_fun/all_to_all | solution.py:211
Sparse Core Ops, SparseCore 0:
  53.0 80.9 all-gather.5

commit v3 on v2

--- a/solution.py
+++ b/solution.py
@@ -13,6 +13,7 @@
 NI = 8
 NJ = 8
 NK = 32
+PACK_J = 4
 BV = 2048
 NB = BV // TILE
 KEEP_CAPS = (18, 20, 24)
@@ -49,13 +50,19 @@
         count = count + jnp.minimum(mask_ref[jt, b], 1)
 
 
+def choose_kernel(mask_ref, o_ref):
+    most = jnp.int32(0)
+    for row in range(mask_ref.shape[0]):
+        most = jnp.maximum(most, sum(mask_ref[row, b] for b in range(NB)))
+    o_ref[0] = sum((most > cap).astype(jnp.int32) for cap in KEEP_CAPS[:-1])
+    o_ref[1] = most
+
+
 def pack_kernel(cap, mask_ref, jt_ref, x_ref, o_ref, xs_ref, idx_ref):
     @pl.when(pl.program_id(0) == 0)
     def _():
         list_kept(mask_ref, jt_ref[0], idx_ref, None)
 
-    xs_ref[...] = x_ref[:, 0].reshape(2 * NK, BV)
-
     def lanes_of(tile):
         return xs_ref[:, pl.ds(pl.multiple_of((tile // 2) * LANES, LANES), LANES)]
 
@@ -66,21 +73,27 @@
         return jnp.where(tile % 2 == 1, v, turn(v, TILE))
 
     first = jt_ref[1]
-    for tile, fold, row, _ in pieces(cap)[0]:
-        for q in range(4):
-            if fold == 1:
-                t0 = idx_ref[first + tile + 2 * q]
-                t1 = idx_ref[first + tile + 2 * q + 1]
-                parts = [low(lanes_of(t0), t0)[:, :TILE], high(lanes_of(t1), t1)[:, TILE:]]
-            elif fold == 2:
-                t0 = idx_ref[first + tile + q]
-                v = lanes_of(t0)
-                parts = [low(v[:32], t0)[:, :TILE], high(v[32:], t0)[:, TILE:]]
-            else:
-                t0 = idx_ref[first + tile + q // 2]
-                v = low(lanes_of(t0), t0)
-                parts = [turn(v[16 * g : 16 * g + 16], 32 * (g - q % 2))[:, 32 * g : 32 * g + 32] for g in range(4)]
-            o_ref[q, row : row + 64 // fold, :] = jnp.concatenate(parts, axis=1)
+
+    def one_j(j, carry):
+        xs_ref[...] = x_ref[:, j].reshape(2 * NK, BV)
+        for tile, fold, row, _ in pieces(cap)[0]:
+            for q in range(4):
+                if fold == 1:
+                    t0 = idx_ref[first + tile + 2 * q]
+                    t1 = idx_ref[first + tile + 2 * q + 1]
+                    parts = [low(lanes_of(t0), t0)[:, :TILE], high(lanes_of(t1), t1)[:, TILE:]]
+                elif fold == 2:
+                    t0 = idx_ref[first + tile + q]
+                    v = lanes_of(t0)
+                    parts = [low(v[:32], t0)[:, :TILE], high(v[32:], t0)[:, TILE:]]
+                else:
+                    t0 = idx_ref[first + tile + q // 2]
+                    v = low(lanes_of(t0), t0)
+                    parts = [turn(v[16 * g : 16 * g + 16], 32 * (g - q % 2))[:, 32 * g : 32 * g + 32] for g in range(4)]
+                o_ref[4 * j + q, row : row + 64 // fold, :] = jnp.concatenate(parts, axis=1)
+        return carry
+
+    lax.fori_loop(0, PACK_J, one_j, 0)
 
 
 def contract_kernel(cap, r_ref, w_ref, o_ref, x_ref):
@@ -173,7 +186,7 @@
     lax.fori_loop(0, NJ, one_j, 0)
 
 
-def one_pass(cap, before, amplitudes, integrals, others, row_term, virtual_right, tile_mask, jt):
+def one_pass(cap, before, amplitudes, integrals, others, levels, tile_mask, jt):
     found, rows_in, rows_out = pieces(cap)
     bf16 = jnp.bfloat16
     whole = pl.BlockSpec(memory_space=pltpu.VMEM)
@@ -183,9 +196,9 @@
         out_shape=jax.ShapeDtypeStruct((ROWS, rows_in, LANES), bf16),
         grid_spec=pltpu.PrefetchScalarGridSpec(
             num_scalar_prefetch=2,
-            grid=(NJ,),
-            in_specs=[pl.BlockSpec((NK, 1, 2, BV), lambda j, m, t: (0, j, 0, 0))],
-            out_specs=pl.BlockSpec((4, rows_in, LANES), lambda j, m, t: (j, 0, 0)),
+            grid=(NJ // PACK_J,),
+            in_specs=[pl.BlockSpec((NK, PACK_J, 2, BV), lambda j, m, t: (0, j, 0, 0))],
+            out_specs=pl.BlockSpec((4 * PACK_J, rows_in, LANES), lambda j, m, t: (j, 0, 0)),
             scratch_shapes=[pltpu.VMEM((2 * NK, BV), bf16), pltpu.SMEM((2 * NB,), jnp.int32)],
         ),
         name="pack",
@@ -210,6 +223,11 @@
     )(received, weights)
     returned = lax.all_to_all(cycle, "row", split_axis=0, concat_axis=0, tiled=True)
 
+    occupied_left, occupied_right, virtual_left, virtual_right = levels
+    row_term = (
+        occupied_left[None, :, None] + occupied_right[:, None, None] - virtual_left[None, None, :]
+    ).reshape(NJ, NI * 2)
+    row_term = jnp.broadcast_to(row_term[:, :, None], (NJ, NI * 2, LANES))
     residual, factor = pl.pallas_call(
         prepare_kernel,
         out_shape=[
@@ -260,15 +278,25 @@
     tile_mask,
 ):
     jt = (lax.axis_index("col") // (TILE // NJ)).astype(jnp.int32)
-    row_term = (
-        occupied_left[None, :, None] + occupied_right[:, None, None] - virtual_left[None, None, :]
-    ).reshape(NJ, NI * 2)
-    row_term = jnp.broadcast_to(row_term[:, :, None], (NJ, NI * 2, LANES))
-    most = jnp.max(jnp.sum(tile_mask, axis=1))
-    branch = sum((most > cap).astype(jnp.int32) for cap in KEEP_CAPS[:-1])
+    chosen = pl.pallas_call(
+        choose_kernel,
+        out_shape=jax.ShapeDtypeStruct((2,), jnp.int32),
+        in_specs=[pl.BlockSpec(memory_space=pltpu.SMEM)],
+        out_specs=pl.BlockSpec(memory_space=pltpu.SMEM),
+        name="choose",
+    )(tile_mask)
+    branch, most = chosen[0], chosen[1]
     steps = [functools.partial(once, cap) for cap in KEEP_CAPS[:-1]] + [functools.partial(repeatedly, KEEP_CAPS[-1])]
     return lax.switch(
-        branch, steps, most, jt, amplitudes, integrals, others, row_term, virtual_right, tile_mask
+        branch,
+        steps,
+        most,
+        jt,
+        amplitudes,
+        integrals,
+        others,
+        (occupied_left, occupied_right, virtual_left, virtual_right),
+        tile_mask,
     )
 
 

time: 244 us -> 239 us (0.980)
  no operation moved by 1% of the time
where the time goes in v3:
time: 239 us; the launch traced here: 238 us
  waiting for transfers between devices  159 us (67%)
  starting transfers between devices  39.9 us (17%)
  between operations  13.4 us (6%)
  Pallas kernels  12.7 us (5%)
  local copies, waits for them, and re-layouts  12 us (5%)
    all_gather x1, waiting for transfers between devices, one_pass(): gathered = lax.all_gather(own, 'col', axis=0, tiled=False)  84.9 us
    all_to_all x1, waiting for transfers between devices, one_pass(): lax.all_to_all(cycle, 'row', split_axis=0, concat_axis=0, tiled=True)  45.6 us
    all_to_all x1, starting transfers between devices, one_pass(): lax.all_to_all(packed, 'row', split_axis=0, concat_axis=0, tiled=True)  29.4 us
    all_to_all x1, waiting for transfers between devices, one_pass(): lax.all_to_all(packed, 'row', split_axis=0, concat_axis=0, tiled=True)  28.6 us
    all_to_all x1, starting transfers between devices, one_pass(): lax.all_to_all(cycle, 'row', split_axis=0, concat_axis=0, tiled=True)  10.2 us
    reshape x2, local copies, waits for them, and re-layouts, one_pass(): gathered.reshape(NK, ROWS, 2, NI * TILE).transpose(1, 0, 2, 3)  5.17 us
  transfers between devices with their start and end apart: 3, of which 3 were waited for; matrix products, arithmetic and copies ran while one was open for 5% of the time, Pallas kernels for 1%

profile of v3, /device:TPU:1, one launch (start us, length us, event | category | flops | bytes accessed | tf_op | source)
XLA Modules:
  0.0 238.1 jit_solution(3733570772654161054)
XLA Ops:
  6.5 1.4 choose.1
  7.9 223.3 %conditional.1 = (bf16[8,8,2,2048]{3,2,1,0:T(2,128)(2,1)}) conditional(s32[]{:T(128)} %bitcast.36, (s32[]{:T(128)}, s32[4,32]{1,0:T(4,128)}, bf16[32,8,2,2048]{3,2,1,0:T(2,128)(2,1)}, bf16[8,64,1,64]{3,1,2,0:T(8,128)(2,1)}, f32[8]{0:T(128)}, /*index=5*/f32[8]{0:T(128)}, f32[2]{0:T(128)}, f32[2048]{0:T(1024)}, ...), branch_computations={%region_0.1_spmd, %region_1.2_spmd, %region_2.5_spmd} | conditional | flops 207 | bytes 33332036 | solution.py:290
  8.0 0.6 pad_add_fusion.1.jt_ref
  8.6 4.7 %pack.4 = bf16[32,160,128]{2,1,0:T(8,128)(2,1)} custom-call(s32[4,32]{1,0:T(4,128)} %get-tuple-element.126.mask_ref, s32[2]{0:T(128)} %pad_add_fusion.1.jt_ref, bf16[32,8,2,2048]{3,2,1,0:T(2,128)(2,1)} %get-tuple-element.128.x_ref), custom_call_target="tpu_custom_call" | custom-call | tf_op jit(solution)/shard_map/cond/branch_1_fun/pack/pallas_call | solution.py:194
  13.2 0.0 copy-start.7
  13.2 29.4 %all-to-all-start.2 = ((bf16[32,160,128]{2,1,0:T(8,128)(2,1)}), bf16[32,160,128]{2,1,0:T(8,128)(2,1)S(1)}, u32[]{:S(2)}, u32[]{:S(2)}) async-start(bf16[32,160,128]{2,1,0:T(8,128)(2,1)} %pack.4), calls=%async_computation.2 | async-start | bytes 2621440 | tf_op jit(solution)/shard_map/cond/branch_1_fun/all_to_all | solution.py:206
  42.6 0.2 all-gather.6.cloned.1.call-start
  42.9 0.0 copy-done.7
  42.9 0.1 copy.55
  43.0 0.1 copy.42
  43.1 0.7 copy.43
  43.8 0.0 all-gather.6.cloned.1.call-update
  43.8 84.9 %all-gather.6.cloned.1.call-done = bf16[32,64,512]{2,1,0:T(8,128)(2,1)} async-done(((bf16[1,64,512]{2,1,0:T(8,128)(2,1)}), bf16[32,64,512]{2,1,0:T(8,128)(2,1)}) %all-gather.6.cloned.1.call-update) | async-done | bytes 2097168 | tf_op jit(solution)/shard_map/cond/branch_1_fun/all_gather | solution.py:209
  128.8 2.8 %copy.44 = bf16[32,64,512]{2,0,1:T(8,128)(2,1)S(1)} copy(bf16[32,64,512]{2,1,0:T(8,128)(2,1)} %all-gather.6.cloned.1.call-done) | data formatting | bytes 4194304 | tf_op jit(solution)/shard_map/cond/branch_1_fun/all_gather | solution.py:209
  131.5 2.2 copy.45
  133.7 2.2 reshape.182
  136.0 2.9 %copy.46 = bf16[2048,512]{0,1:T(8,128)(2,1)S(1)} copy(bf16[2048,512]{1,0:T(8,128)(2,1)} %reshape.182) | data formatting | bytes 4194304 | tf_op jit(solution)/shard_map/cond/branch_1_fun/reshape | solution.py:210
  138.9 28.6 %all-to-all-done.2.r_ref = bf16[32,160,128]{2,1,0:T(8,128)(2,1)S(1)} async-done(((bf16[32,160,128]{2,1,0:T(8,128)(2,1)}), bf16[32,160,128]{2,1,0:T(8,128)(2,1)S(1)}, u32[]{:S(2)}, u32[]{:S(2)}) %all-to-all-start.2) | async-done | bytes 1310752 | tf_op jit(solution)/shard_map/cond/branch_1_fun/all_to_all | solution.py:206
  167.5 0.0 copy-start.21
  167.5 0.0 copy-start.15
  167.5 0.0 copy-start.18
  167.5 0.0 copy-start.4
  167.5 0.0 copy-start.9
  167.5 0.0 copy-start.12
  167.6 1.5 contract.4
  169.0 0.0 copy-start
  169.1 0.7 copy-done
  169.8 10.2 %all-to-all-start.3 = ((bf16[32,40,128]{2,1,0:T(8,128)(2,1)}), bf16[32,40,128]{2,1,0:T(8,128)(2,1)S(1)}, u32[]{:S(2)}, u32[]{:S(2)}) async-start(bf16[32,40,128]{2,1,0:T(8,128)(2,1)} %copy-done), calls=%async_computation.3 | async-start | bytes 655360 | tf_op jit(solution)/shard_map/cond/branch_1_fun/all_to_all | solution.py:224
  180.0 0.0 copy-done.21
  180.0 0.1 sub.67
  180.1 0.0 copy-done.15
  180.1 0.0 copy-done.18
  180.1 0.1 broadcast_add_fusion.1
  180.2 0.1 broadcast_subtract_fusion.1
  180.3 0.1 copy.47
  180.3 0.1 broadcast_in_dim.15.row_ref
  180.4 0.0 copy-done.4
  180.4 0.0 copy-done.9
  180.4 0.0 copy-done.12
  180.4 1.3 prepare.4
  181.8 45.6 %all-to-all-done.3.c_ref = bf16[32,40,128]{2,1,0:T(8,128)(2,1)S(1)} async-done(((bf16[32,40,128]{2,1,0:T(8,128)(2,1)}), bf16[32,40,128]{2,1,0:T(8,128)(2,1)S(1)}, u32[]{:S(2)}, u32[]{:S(2)}) %all-to-all-start.3) | async-done | bytes 327712 | tf_op jit(solution)/shard_map/cond/branch_1_fun/all_to_all | solution.py:224
  227.4 3.8 %update.4 = bf16[8,8,2,2048]{3,2,1,0:T(2,128)(2,1)} custom-call(s32[4,32]{1,0:T(4,128)S(1)} %copy-done.9, s32[2]{0:T(128)S(1)} %copy-done.4, bf16[32,40,128]{2,1,0:T(8,128)(2,1)S(1)} %all-to-all-done.3.c_ref, bf16[8,16,2048]{2,1,0:T(8,128)(2,1)S(1)} %get-tuple-element.135.oths_ref, f32[8,16,2048]{2,1,0:T(8,128)S(1)} %get-tuple-element.136.factor_ref), custom_call_target="tpu_custom_call" | custom-call | tf_op jit(solution)/shard_map/cond/branch_1_fun/update/pallas_call | solution.py:243
  (2 shorter events, 0.0 us)
Async XLA Ops:
  13.2 29.7 %copy-start.7 = (bf16[8,64,1,64]{3,1,2,0:T(8,128)(2,1)S(1)}, bf16[8,64,1,64]{3,1,2,0:T(8,128)(2,1)}, u32[]{:S(2)}) copy-start(bf16[8,64,1,64]{3,1,2,0:T(8,128)(2,1)} %get-tuple-element.233) | copy-start | bytes 196612 | tf_op jit(solution)/shard_map/cond
  13.2 154.3 %all-to-all-start.2 = ((bf16[32,160,128]{2,1,0:T(8,128)(2,1)}), bf16[32,160,128]{2,1,0:T(8,128)(2,1)S(1)}, u32[]{:S(2)}, u32[]{:S(2)}) async-start(bf16[32,160,128]{2,1,0:T(8,128)(2,1)} %pack.4), calls=%async_computation.2 | async-start | bytes 2621440 | tf_op jit(solution)/shard_map/cond/branch_1_fun/all_to_all | solution.py:206
  42.6 86.1 %all-gather.6.cloned.1.call-start = ((), (), s32[]{:S(2)}) async-start(), calls=%async_computation.7 | async-start | bytes 2162688 | tf_op jit(solution)/shard_map/cond/branch_1_fun/all_gather | solution.py:209
  167.5 12.5 %copy-start.21 = (f32[2]{0:T(128)S(1)}, f32[2]{0:T(128)}, u32[]{:S(2)}) copy-start(f32[2]{0:T(128)} %get-tuple-element.133) | copy-start | bytes 28 | tf_op jit(solution)/shard_map/cond
  167.5 12.6 %copy-start.15 = (f32[8]{0:T(128)S(1)}, f32[8]{0:T(128)}, u32[]{:S(2)}) copy-start(f32[8]{0:T(128)} %get-tuple-element.131) | copy-start | bytes 100 | tf_op jit(solution)/shard_map/cond
  167.5 12.6 %copy-start.18 = (f32[8]{0:T(128)S(1)}, f32[8]{0:T(128)}, u32[]{:S(2)}) copy-start(f32[8]{0:T(128)} %get-tuple-element.132) | copy-start | bytes 100 | tf_op jit(solution)/shard_map/cond
  167.5 12.9 %copy-start.4 = (s32[2]{0:T(128)S(1)}, s32[2]{0:T(128)}, u32[]{:S(2)}) copy-start(s32[2]{0:T(128)} %pad_add_fusion.1.jt_ref) | copy-start | bytes 28 | tf_op jit(solution)/shard_map/cond
  167.5 12.9 %copy-start.9 = (s32[4,32]{1,0:T(4,128)S(1)}, s32[4,32]{1,0:T(4,128)}, u32[]{:S(2)}) copy-start(s32[4,32]{1,0:T(4,128)} %get-tuple-element.126.mask_ref) | copy-start | bytes 1540 | tf_op jit(solution)/shard_map/cond
  167.5 12.9 %copy-start.12 = (f32[2048]{0:T(1024)S(1)}, f32[2048]{0:T(1024)}, u32[]{:S(2)}) copy-start(f32[2048]{0:T(1024)} %get-tuple-element.134) | copy-start | bytes 24580 | tf_op jit(solution)/shard_map/cond
  169.0 0.7 copy-start
  169.8 57.6 %all-to-all-start.3 = ((bf16[32,40,128]{2,1,0:T(8,128)(2,1)}), bf16[32,40,128]{2,1,0:T(8,128)(2,1)S(1)}, u32[]{:S(2)}, u32[]{:S(2)}) async-start(bf16[32,40,128]{2,1,0:T(8,128)(2,1)} %copy-done), calls=%async_computation.3 | async-start | bytes 655360 | tf_op jit(solution)/shard_map/cond/branch_1_fun/all_to_all | solution.py:224
Sparse Core Ops, SparseCore 0:
  47.8 80.9 all-gather.5

commit v4 on v3

--- a/solution.py
+++ b/solution.py
@@ -58,7 +58,10 @@
     o_ref[1] = most
 
 
-def pack_kernel(cap, mask_ref, jt_ref, x_ref, o_ref, xs_ref, idx_ref):
+def pack_kernel(cap, repeated, mask_ref, jt_ref, *refs):
+    first = refs[0][0] if repeated else 0
+    x_ref, o_ref, xs_ref, idx_ref = refs[repeated:]
+
     @pl.when(pl.program_id(0) == 0)
     def _():
         list_kept(mask_ref, jt_ref[0], idx_ref, None)
@@ -71,8 +74,6 @@
 
     def high(v, tile):
         return jnp.where(tile % 2 == 1, v, turn(v, TILE))
-
-    first = jt_ref[1]
 
     def one_j(j, carry):
         xs_ref[...] = x_ref[:, j].reshape(2 * NK, BV)
@@ -137,11 +138,12 @@
     lax.fori_loop(0, NJ, one_j, 0)
 
 
-def update_kernel(cap, repeated, mask_ref, jt_ref, c_ref, oths_ref, factor_ref, *refs):
+def update_kernel(cap, repeated, mask_ref, jt_ref, *refs):
+    first = refs[0][0] if repeated else 0
+    c_ref, oths_ref, factor_ref, *refs = refs[repeated:]
     if repeated:
         before_ref, *refs = refs
     o_ref, comp_ref, res_ref, pos_ref = refs
-    first = jt_ref[1]
     found = pieces(cap)[0]
     list_kept(mask_ref, jt_ref[0], None, pos_ref)
     low = lane_group((16, LANES), TILE) == 0
@@ -183,26 +185,27 @@
         o_ref[:, j] = res_ref[...].reshape(NI, 2, BV).astype(jnp.bfloat16)
         return carry
 
-    lax.fori_loop(0, NJ, one_j, 0)
-
-
-def one_pass(cap, before, amplitudes, integrals, others, levels, tile_mask, jt):
+    lax.fori_loop(0, NJ, one_j, 0, unroll=2)
+
+
+def one_pass(cap, first, before, amplitudes, integrals, others, levels, tile_mask, jt):
     found, rows_in, rows_out = pieces(cap)
     bf16 = jnp.bfloat16
+    repeated = len(first)
     whole = pl.BlockSpec(memory_space=pltpu.VMEM)
     scalars = pl.BlockSpec(memory_space=pltpu.SMEM)
     packed = pl.pallas_call(
-        functools.partial(pack_kernel, cap),
+        functools.partial(pack_kernel, cap, repeated),
         out_shape=jax.ShapeDtypeStruct((ROWS, rows_in, LANES), bf16),
         grid_spec=pltpu.PrefetchScalarGridSpec(
-            num_scalar_prefetch=2,
+            num_scalar_prefetch=2 + repeated,
             grid=(NJ // PACK_J,),
-            in_specs=[pl.BlockSpec((NK, PACK_J, 2, BV), lambda j, m, t: (0, j, 0, 0))],
-            out_specs=pl.BlockSpec((4 * PACK_J, rows_in, LANES), lambda j, m, t: (j, 0, 0)),
+            in_specs=[pl.BlockSpec((NK, PACK_J, 2, BV), lambda j, *_: (0, j, 0, 0))],
+            out_specs=pl.BlockSpec((4 * PACK_J, rows_in, LANES), lambda j, *_: (j, 0, 0)),
             scratch_shapes=[pltpu.VMEM((2 * NK, BV), bf16), pltpu.SMEM((2 * NB,), jnp.int32)],
         ),
         name="pack",
-    )(tile_mask, jt, amplitudes)
+    )(tile_mask, jt, *first, amplitudes)
     received = lax.all_to_all(packed, "row", split_axis=0, concat_axis=0, tiled=True)
 
     own = integrals[:, :, 0, :].reshape(NI, ROWS, 2, TILE).transpose(3, 1, 0, 2).reshape(TILE, NI * TILE)
@@ -241,9 +244,9 @@
     )(tile_mask, jt, others, row_term, virtual_right[None])
 
     return pl.pallas_call(
-        functools.partial(update_kernel, cap, bool(before)),
+        functools.partial(update_kernel, cap, repeated),
         out_shape=jax.ShapeDtypeStruct(others.shape, bf16),
-        in_specs=[scalars, scalars, whole, whole, whole] + [whole] * len(before),
+        in_specs=[scalars] * (2 + repeated) + [whole] * (3 + len(before)),
         out_specs=whole,
         scratch_shapes=[
             pltpu.VMEM((cap // 2, 16, LANES), jnp.float32),
@@ -252,19 +255,19 @@
         ],
         compiler_params=pltpu.CompilerParams(vmem_limit_bytes=40 << 20),
         name="update",
-    )(tile_mask, jt, returned, residual, factor, *before)
+    )(tile_mask, jt, *first, returned, residual, factor, *before)
 
 
 def once(cap, most, jt, *arrays):
-    return one_pass(cap, [], *arrays, jnp.stack([jt, jnp.int32(0)]))
+    return one_pass(cap, [], [], *arrays, jt)
 
 
 def repeatedly(cap, most, jt, *arrays):
     def step(n, before):
-        return one_pass(cap, [before], *arrays, jnp.stack([jt, n * cap]))
+        return one_pass(cap, [(n * cap).reshape(1)], [before], *arrays, jt)
 
     passes = jnp.maximum((most + cap - 1) // cap, 1)
-    return lax.fori_loop(0, passes, step, jnp.zeros_like(arrays[2]))
+    return lax.fori_loop(0, passes, step, arrays[2])
 
 
 def shards(
@@ -277,7 +280,7 @@
     virtual_right,
     tile_mask,
 ):
-    jt = (lax.axis_index("col") // (TILE // NJ)).astype(jnp.int32)
+    jt = (lax.axis_index("col") // (TILE // NJ)).astype(jnp.int32).reshape(1)
     chosen = pl.pallas_call(
         choose_kernel,
         out_shape=jax.ShapeDtypeStruct((2,), jnp.int32),

time: 239 us -> 227 us (0.950)
  waiting for transfers between devices: 159 us -> 150 us
    all_to_all x1, waiting for transfers between devices: 28.6 us -> 19.2 us  [one_pass(): lax.all_to_all(packed, 'row', split_axis=0, concat_axis=0, tiled=True)]
where the time goes in v4:
time: 227 us; the launch traced here: 226 us
  waiting for transfers between devices  150 us (66%)
  starting transfers between devices  37.7 us (17%)
  between operations  13.4 us (6%)
  Pallas kernels  12.8 us (6%)
  local copies, waits for them, and re-layouts  12 us (5%)
    all_gather x1, waiting for transfers between devices, one_pass(): gathered = lax.all_gather(own, 'col', axis=0, tiled=False)  85.1 us
    all_to_all x1, waiting for transfers between devices, one_pass(): lax.all_to_all(cycle, 'row', split_axis=0, concat_axis=0, tiled=True)  45.6 us
    all_to_all x1, starting transfers between devices, one_pass(): lax.all_to_all(packed, 'row', split_axis=0, concat_axis=0, tiled=True)  29.3 us
    all_to_all x1, waiting for transfers between devices, one_pass(): lax.all_to_all(packed, 'row', split_axis=0, concat_axis=0, tiled=True)  19.2 us
    all_to_all x1, starting transfers between devices, one_pass(): lax.all_to_all(cycle, 'row', split_axis=0, concat_axis=0, tiled=True)  8.4 us
    reshape x2, local copies, waits for them, and re-layouts, one_pass(): gathered.reshape(NK, ROWS, 2, NI * TILE).transpose(1, 0, 2, 3)  5.18 us
    pallas_call x1, Pallas kernels, one_pass(): pl.pallas_call(functools.partial(pack_kernel, cap, repeated), out_shape=j...  4.76 us
  transfers between devices with their start and end apart: 3, of which 3 were waited for; matrix products, arithmetic and copies ran while one was open for 5% of the time, Pallas kernels for 1%

profile of v4, /device:TPU:1, one launch (start us, length us, event | category | flops | bytes accessed | tf_op | source)
XLA Modules:
  0.0 226.3 jit_solution(10778364815143483291)
XLA Ops:
  6.5 1.4 choose.1
  7.9 211.5 %conditional.1 = (bf16[8,8,2,2048]{3,2,1,0:T(2,128)(2,1)}) conditional(s32[]{:T(128)} %bitcast.33, (s32[4,32]{1,0:T(4,128)}, s32[1]{0:T(128)}, bf16[32,8,2,2048]{3,2,1,0:T(2,128)(2,1)}, bf16[8,64,1,64]{3,1,2,0:T(8,128)(2,1)}, f32[8]{0:T(128)}, /*index=5*/f32[8]{0:T(128)}, f32[2]{0:T(128)}, f32[2048]{0:T(1024)}, ...), branch_computations={%region_0.1_spmd, %region_1.2_spmd, %region_2.5_spmd} | conditional | flops 205 | bytes 33856248 | solution.py:293
  8.0 0.0 copy-start.3
  8.0 4.8 %pack.3 = bf16[32,144,128]{2,1,0:T(8,128)(2,1)} custom-call(s32[4,32]{1,0:T(4,128)} %get-tuple-element.115.mask_ref, s32[1]{0:T(128)} %get-tuple-element.116.jt_ref, bf16[32,8,2,2048]{3,2,1,0:T(2,128)(2,1)} %get-tuple-element.117.refs_0_), custom_call_target="tpu_custom_call" | custom-call | tf_op jit(solution)/shard_map/cond/branch_0_fun/pack/pallas_call | solution.py:197
  12.7 29.3 %all-to-all-start = ((bf16[32,144,128]{2,1,0:T(8,128)(2,1)}), bf16[32,144,128]{2,1,0:T(8,128)(2,1)S(1)}, u32[]{:S(2)}, u32[]{:S(2)}) async-start(bf16[32,144,128]{2,1,0:T(8,128)(2,1)} %pack.3), calls=%async_computation | async-start | bytes 2359296 | tf_op jit(solution)/shard_map/cond/branch_0_fun/all_to_all | solution.py:209
  42.0 0.0 all-gather.4.cloned.1.call-start
  42.1 0.0 copy-done.3
  42.1 0.1 copy.54
  42.2 0.1 copy.36
  42.3 0.7 copy.37
  43.0 0.0 all-gather.4.cloned.1.call-update
  43.0 85.1 %all-gather.4.cloned.1.call-done = bf16[32,64,512]{2,1,0:T(8,128)(2,1)} async-done(((bf16[1,64,512]{2,1,0:T(8,128)(2,1)}), bf16[32,64,512]{2,1,0:T(8,128)(2,1)}) %all-gather.4.cloned.1.call-update) | async-done | bytes 2097168 | tf_op jit(solution)/shard_map/cond/branch_0_fun/all_gather | solution.py:212
  128.2 2.8 %copy.38 = bf16[32,64,512]{2,0,1:T(8,128)(2,1)S(1)} copy(bf16[32,64,512]{2,1,0:T(8,128)(2,1)} %all-gather.4.cloned.1.call-done) | data formatting | bytes 4194304 | tf_op jit(solution)/shard_map/cond/branch_0_fun/all_gather | solution.py:212
  130.9 2.2 copy.39
  133.1 2.3 reshape.183
  135.4 2.9 %copy.40 = bf16[2048,512]{0,1:T(8,128)(2,1)S(1)} copy(bf16[2048,512]{1,0:T(8,128)(2,1)} %reshape.183) | data formatting | bytes 4194304 | tf_op jit(solution)/shard_map/cond/branch_0_fun/reshape | solution.py:213
  138.3 19.2 %all-to-all-done.r_ref = bf16[32,144,128]{2,1,0:T(8,128)(2,1)S(1)} async-done(((bf16[32,144,128]{2,1,0:T(8,128)(2,1)}), bf16[32,144,128]{2,1,0:T(8,128)(2,1)S(1)}, u32[]{:S(2)}, u32[]{:S(2)}) %all-to-all-start) | async-done | bytes 1179680 | tf_op jit(solution)/shard_map/cond/branch_0_fun/all_to_all | solution.py:209
  157.5 0.0 copy-start.17
  157.5 0.0 copy-start.11
  157.5 0.0 copy-start.14
  157.5 0.0 copy-start.5
  157.5 0.0 copy-start.8
  157.5 1.5 contract.3
  159.1 0.0 copy-start.1
  159.1 0.7 copy-done.1
  159.8 8.4 %all-to-all-start.1 = ((bf16[32,36,128]{2,1,0:T(8,128)(2,1)}), bf16[32,36,128]{2,1,0:T(8,128)(2,1)S(1)}, u32[]{:S(2)}, u32[]{:S(2)}) async-start(bf16[32,36,128]{2,1,0:T(8,128)(2,1)} %copy-done.1), calls=%async_computation.1 | async-start | bytes 655360 | tf_op jit(solution)/shard_map/cond/branch_0_fun/all_to_all | solution.py:227
  168.2 0.0 copy-done.17
  168.2 0.1 sub.61
  168.3 0.0 copy-done.11
  168.3 0.0 copy-done.14
  168.3 0.1 broadcast_add_fusion
  168.4 0.1 broadcast_subtract_fusion
  168.5 0.1 copy.41
  168.5 0.1 broadcast_in_dim.5.row_ref
  168.6 0.0 copy-done.5
  168.6 0.0 copy-done.8
  168.6 1.3 prepare.3
  170.0 45.6 %all-to-all-done.1.refs_0_ = bf16[32,36,128]{2,1,0:T(8,128)(2,1)S(1)} async-done(((bf16[32,36,128]{2,1,0:T(8,128)(2,1)}), bf16[32,36,128]{2,1,0:T(8,128)(2,1)S(1)}, u32[]{:S(2)}, u32[]{:S(2)}) %all-to-all-start.1) | async-done | bytes 294944 | tf_op jit(solution)/shard_map/cond/branch_0_fun/all_to_all | solution.py:227
  215.6 3.8 %update.3 = bf16[8,8,2,2048]{3,2,1,0:T(2,128)(2,1)} custom-call(s32[4,32]{1,0:T(4,128)S(1)} %copy-done.5, s32[1]{0:T(128)} %get-tuple-element.116.jt_ref, bf16[32,36,128]{2,1,0:T(8,128)(2,1)S(1)} %all-to-all-done.1.refs_0_, bf16[8,16,2048]{2,1,0:T(8,128)(2,1)S(1)} %get-tuple-element.124.refs_1_, f32[8,16,2048]{2,1,0:T(8,128)S(1)} %get-tuple-element.125.refs_2_), custom_call_target="tpu_custom_call" | custom-call | tf_op jit(solution)/shard_map/cond/branch_0_fun/update/pallas_call | solution.py:246
  (2 shorter events, 0.0 us)
Async XLA Ops:
  8.0 34.1 %copy-start.3 = (bf16[8,64,1,64]{3,1,2,0:T(8,128)(2,1)S(1)}, bf16[8,64,1,64]{3,1,2,0:T(8,128)(2,1)}, u32[]{:S(2)}) copy-start(bf16[8,64,1,64]{3,1,2,0:T(8,128)(2,1)} %get-tuple-element.224) | copy-start | bytes 196612 | tf_op jit(solution)/shard_map/cond
  12.7 144.8 %all-to-all-start = ((bf16[32,144,128]{2,1,0:T(8,128)(2,1)}), bf16[32,144,128]{2,1,0:T(8,128)(2,1)S(1)}, u32[]{:S(2)}, u32[]{:S(2)}) async-start(bf16[32,144,128]{2,1,0:T(8,128)(2,1)} %pack.3), calls=%async_computation | async-start | bytes 2359296 | tf_op jit(solution)/shard_map/cond/branch_0_fun/all_to_all | solution.py:209
  42.0 86.1 %all-gather.4.cloned.1.call-start = ((), (), s32[]{:S(2)}) async-start(), calls=%async_computation.6 | async-start | bytes 2162688 | tf_op jit(solution)/shard_map/cond/branch_0_fun/all_gather | solution.py:212
  157.5 10.7 %copy-start.17 = (f32[2]{0:T(128)S(1)}, f32[2]{0:T(128)}, u32[]{:S(2)}) copy-start(f32[2]{0:T(128)} %get-tuple-element.122) | copy-start | bytes 28 | tf_op jit(solution)/shard_map/cond
  157.5 10.8 %copy-start.11 = (f32[8]{0:T(128)S(1)}, f32[8]{0:T(128)}, u32[]{:S(2)}) copy-start(f32[8]{0:T(128)} %get-tuple-element.120) | copy-start | bytes 100 | tf_op jit(solution)/shard_map/cond
  157.5 10.8 %copy-start.14 = (f32[8]{0:T(128)S(1)}, f32[8]{0:T(128)}, u32[]{:S(2)}) copy-start(f32[8]{0:T(128)} %get-tuple-element.121) | copy-start | bytes 100 | tf_op jit(solution)/shard_map/cond
  157.5 11.1 %copy-start.5 = (s32[4,32]{1,0:T(4,128)S(1)}, s32[4,32]{1,0:T(4,128)}, u32[]{:S(2)}) copy-start(s32[4,32]{1,0:T(4,128)} %get-tuple-element.115.mask_ref) | copy-start | bytes 1540 | tf_op jit(solution)/shard_map/cond
  157.5 11.1 %copy-start.8 = (f32[2048]{0:T(1024)S(1)}, f32[2048]{0:T(1024)}, u32[]{:S(2)}) copy-start(f32[2048]{0:T(1024)} %get-tuple-element.123) | copy-start | bytes 24580 | tf_op jit(solution)/shard_map/cond
  159.1 0.7 copy-start.1
  159.8 55.8 %all-to-all-start.1 = ((bf16[32,36,128]{2,1,0:T(8,128)(2,1)}), bf16[32,36,128]{2,1,0:T(8,128)(2,1)S(1)}, u32[]{:S(2)}, u32[]{:S(2)}) async-start(bf16[32,36,128]{2,1,0:T(8,128)(2,1)} %copy-done.1), calls=%async_computation.1 | async-start | bytes 655360 | tf_op jit(solution)/shard_map/cond/branch_0_fun/all_to_all | solution.py:227
Sparse Core Ops, SparseCore 0:
  47.2 80.9 all-gather.3
